TPU v7x, 32 devices: a whole 2x2x4 slice. The times are simulated.
32 devices in a mesh: aux: 8 (over y, x, core), orb: 4 (over z).
Axes of the slice: x: 2, y: 2, z: 4, core: 2. Of those that a mesh axis runs over, the one named last changes fastest.
Arguments:
- band_pattern: int32 [64, 4], P('aux'), may hold values 0 or 1
- density_in: bfloat16 [64, 4, 128, 128], P('aux', 'orb')
- field_terms: bfloat16 [2, 64, 4, 128, 128], P(None, 'aux', 'orb'), may hold values from -3 to 3
- fit_blocks: int32 [1], replicated, may hold values from 0 to 63
- tensor: bfloat16 [1, 3072, 4, 16384], P(None, 'aux', 'orb'), may hold values from -0.0234375 to 0.0234375
- metric_inv: float32 [1, 3072, 3072], P(None, 'aux')
Outputs:
- response: bfloat16 [2, 64, 4, 128, 128], P(None, 'aux', 'orb')
- coefficients: float32 [1, 2, 3072], P(None, None, 'aux')
All inputs are finite; a program needn't handle non-finite values. No bound on the sum of `band_pattern` on one device may be relied on, other than what follows from the above.
Results may differ from a plain program's by a relative error of at most 0.0055.
Values may be sent and summed in bfloat16 or wider, within the bound.
No kernel may reach another device: no remote copies, remote signals or barrier semaphores. Data moves between devices by JAX's collectives and lax.ppermute only.
A program may use at most 192 MiB of HBM per device.

v0:
```python
import jax
import jax.numpy as jnp
from jax import lax
from jax.sharding import PartitionSpec as P


def padded_2(block, sides, width):
    for axis, dim in sides:
        count = lax.axis_size(axis)
        forward = [(i, i + 1) for i in range(count - 1)]
        backward = [(target, source) for source, target in forward]
        low = lax.ppermute(
            lax.slice_in_dim(block, block.shape[dim] - width, None, axis=dim), axis, forward
        )
        high = lax.ppermute(lax.slice_in_dim(block, 0, width, axis=dim), axis, backward)
        block = jnp.concatenate([low, block, high], axis=dim)
    return block


def from_root(value, axis, source):
    kept = jnp.where(lax.axis_index(axis) == source, value, 0).astype(value.dtype)
    return lax.psum(kept, axis)


def slide_slots(blocks, offset):
    slot_count = blocks.shape[2]
    if offset >= 0:
        padded = jnp.pad(blocks, ((0, 0), (0, 0), (offset, 0), (0, 0), (0, 0)))
        return padded[:, :, :slot_count]
    padded = jnp.pad(blocks, ((0, 0), (0, 0), (0, -offset), (0, 0), (0, 0)))
    return padded[:, :, -offset : -offset + slot_count]


def band_keep(band_pattern, first_row, total_rows):
    slot_count = band_pattern.shape[1]
    half_band = slot_count // 2
    row_ids = first_row + jnp.arange(band_pattern.shape[0], dtype=jnp.int32)[:, None]
    columns = row_ids + jnp.arange(slot_count, dtype=jnp.int32)[None, :] - half_band
    return (band_pattern == 1) & (columns >= 0) & (columns < total_rows)


def own_slot_product(factor_left, right_rims, my_slot):
    count_rows = factor_left.shape[1]
    slot_count = factor_left.shape[2]
    half_band = slot_count // 2
    lead_count = right_rims.shape[0]
    total = None
    for stride in range(slot_count):
        source_slot = my_slot - stride + half_band
        inside = (source_slot >= 0) & (source_slot < slot_count)
        starts = (
            jnp.int32(0),
            jnp.int32(stride),
            jnp.clip(source_slot, 0, slot_count - 1),
            jnp.int32(0),
            jnp.int32(0),
        )
        sizes = (lead_count, count_rows, 1, right_rims.shape[3], right_rims.shape[4])
        picked = lax.dynamic_slice(right_rims, starts, sizes)[:, :, 0]
        picked = jnp.where(inside, picked, jnp.zeros((), picked.dtype))
        product = jnp.matmul(factor_left[:, :, stride], picked, preferred_element_type=jnp.float32)
        total = product if total is None else total + product
    return total


def all_slot_product(factor_left, right_rims):
    count_rows = factor_left.shape[1]
    slot_count = factor_left.shape[2]
    half_band = slot_count // 2
    total = None
    for stride in range(slot_count):
        source = slide_slots(right_rims[:, stride : stride + count_rows], stride - half_band)
        product = jnp.matmul(
            factor_left[:, :, stride : stride + 1], source, preferred_element_type=jnp.float32
        )
        total = product if total is None else total + product
    return total


def rim_fields(field_rows, half_band):
    return padded_2(field_rows, (("aux", 1),), half_band)


def on_device(band_pattern, density_in, field_terms, fit_blocks, tensor, metric_inv):
    count_rows = density_in.shape[0]
    slot_count = lax.axis_size("orb")
    half_band = slot_count // 2
    total_rows = count_rows * lax.axis_size("aux")
    first_row = lax.axis_index("aux") * count_rows
    my_slot = lax.axis_index("orb")
    keep_all = band_keep(band_pattern, first_row, total_rows)
    keep_own = lax.dynamic_index_in_dim(keep_all, my_slot, 1, keepdims=True)[None, :, :, None, None]
    keep_out = keep_own[:, :, 0]
    zero_half = jnp.zeros((), jnp.bfloat16)
    density = jnp.where(keep_own, density_in[None], zero_half)
    perturbed = jnp.where(keep_own, field_terms, zero_half)
    stacked = jnp.concatenate([density, perturbed], 0)
    whole_rows = lax.all_gather(stacked, "orb", axis=2, tiled=True)
    deep_rows = padded_2(whole_rows[0:1], (("aux", 1),), 2 * half_band)
    field_rows = rim_fields(whole_rows[1:], half_band)
    pattern_wide = padded_2(band_pattern, (("aux", 0),), half_band)
    keep_wide = band_keep(pattern_wide, first_row - half_band, total_rows)[None, :, :, None, None]
    density_rims = deep_rows[:, half_band : half_band + count_rows + 2 * half_band]
    cross_term = own_slot_product(whole_rows[0:1], field_rows, my_slot)
    right_term = own_slot_product(whole_rows[1:], density_rims, my_slot)
    first_order = jnp.where(keep_out, cross_term + right_term, 0.0).astype(jnp.bfloat16)
    square_wide = all_slot_product(density_rims, deep_rows)
    square_rims = jnp.where(keep_wide, square_wide, 0.0).astype(jnp.bfloat16)
    square_rows = square_rims[:, half_band : half_band + count_rows]
    order_rows = lax.all_gather(first_order[:, :, None], "orb", axis=2, tiled=True)
    order_rims = rim_fields(order_rows, half_band)
    second = own_slot_product(square_rows, order_rims, my_slot) + own_slot_product(
        order_rows, square_rims, my_slot
    )
    response = jnp.where(keep_out, 2.0 * first_order.astype(jnp.float32) - second, 0.0).astype(
        jnp.bfloat16
    )[:, :, None]
    owner_row = fit_blocks // count_rows
    local_row = fit_blocks % count_rows
    own_piece = lax.dynamic_index_in_dim(response, local_row[0], 1, keepdims=False)
    pieces = [from_root(own_piece, "aux", owner_row[0])]
    fitted = jnp.stack(pieces, 1)
    flat_blocks = fitted.reshape(fitted.shape[0], fitted.shape[1], -1)
    integrals = tensor.reshape(tensor.shape[0], tensor.shape[1], -1)
    partial_value = jnp.einsum(
        "kfm,fpm->fkp", flat_blocks, integrals, preferred_element_type=jnp.float32
    )
    summed = lax.psum(partial_value, "orb")
    full_sums = lax.all_gather(summed, "aux", axis=2, tiled=True)
    coefficients = jnp.einsum(
        "fpq,fkq->fkp", metric_inv, full_sums, precision=lax.Precision.HIGHEST
    )
    return (response, coefficients)


def solution(mesh):
    in_specs = (
        P("aux", None),
        P("aux", "orb", None, None),
        P(None, "aux", "orb", None, None),
        P(),
        P(None, "aux", "orb", None),
        P(None, "aux", None),
    )
    out_specs = (P(None, "aux", "orb", None, None), P(None, None, "aux"))
    return jax.shard_map(
        on_device, mesh=mesh, in_specs=in_specs, out_specs=out_specs, check_vma=False
    )
```

profile of v0, /device:TPU:0, one launch (start us, length us, event | category | flops | bytes accessed | tf_op | source)
XLA Modules:
  0.0 267.4 jit_solution(12053196933223131960)
XLA Ops:
  7.2 0.7 fusion.140
  7.9 1.1 copy_select_fusion
  9.1 1.0 bitcast_select_fusion
  10.2 0.9 copy.31
  11.2 66.3 %all-gather.4.cloned.1.call-done = bf16[3,8,4,128,128]{4,3,1,0,2:T(8,128)(2,1)} async-done(((bf16[3,8,1,128,128]{4,3,1,0,2:T(8,128)(2,1)}), bf16[3,8,4,128,128]{4,3,1,0,2:T(8,128)(2,1)}) %all-gather.4.cloned.1.call-update) | async-done | bytes 3145744 | tf_op jit(solution)/shard_map/all_gather | solution.py:98
  77.5 1.3 slice_bitcast_fusion.10
  78.8 1.6 collective-permute-start.2
  80.4 1.6 collective-permute-start.3
  82.0 1.3 fusion.173
  83.3 4.5 %collective-permute-start = (bf16[2,2,4,128,128]{4,3,0,1,2:T(8,128)(2,1)S(1)}, bf16[2,2,4,128,128]{4,3,0,1,2:T(8,128)(2,1)S(1)}, u32[]{:S(2)}, u32[]{:S(2)}) collective-permute-start(bf16[2,2,4,128,128]{4,3,0,1,2:T(8,128)(2,1)S(1)} %copy.88), channel_id=1, source_target_pairs={{0,4},{4,8},{8,12},{12,16},{16,20},{20,24},{24,28},{1,5},{5,9},{9,... | collective-permute-start | bytes 1572872 | tf_op jit(solution)/shard_map/ppermute | solution.py:12
  87.8 1.3 collective-permute-start.1
  89.5 0.8 copy-done.6
  90.5 2.9 %fusion.174 = (bf16[1,12,4,128,128]{4,3,0,1,2:T(8,128)(2,1)}, bf16[12,4,128,128]{3,2,0,1:T(8,128)(2,1)}, bf16[1,12,4,128,128]{4,3,0,1,2:T(8,128)(2,1)}, bf16[1,12,4,128,128]{4,3,0,1,2:T(8,128)(2,1)S(1)}) fusion(bf16[1,16,4,128,128]{4,3,0,1,2:T(8,128)(2,1)S(1)} %pad_maximum_fusion), kind=kLoop, calls=%fused_computation.228 | loop fusion | bytes 11010048 | tf_op jit(solution)/shard_map/slice | solution.py:72
  93.6 0.3 convolution_add_fusion.8
  93.9 0.3 convolution_add_fusion.7
  95.0 0.3 convolution_add_fusion.11
  95.3 0.3 convolution_add_fusion.10
  95.6 0.3 fusion.25
  95.9 1.1 fusion.27
  97.2 14.1 %collective-permute-start.4 = (s32[2,4]{0,1:T(4,128)S(1)}, s32[2,4]{0,1:T(4,128)S(1)}, u32[]{:S(2)}, u32[]{:S(2)}) collective-permute-start(s32[2,4]{0,1:T(4,128)S(1)} %get-tuple-element.22), channel_id=1, source_target_pairs={{0,4},{4,8},{8,12},{12,16},{16,20},{20,24},{24,28},{1,5},{5,9},{9,... | collective-permute-start | bytes 104 | tf_op jit(solution)/shard_map/ppermute | solution.py:12
  111.3 1.3 collective-permute-start.5
  113.3 1.0 collective-permute-done.5
  114.6 1.9 fusion.13
  116.5 0.4 fusion.15
  116.9 0.9 copy-done.3
  117.9 0.6 fusion.11
  118.5 0.8 copy-done.4
  119.3 1.9 select_convert_fusion
  121.2 31.2 %all-gather.6.cloned.1.call-done = bf16[2,8,512,128]{3,2,0,1:T(8,128)(2,1)} async-done(((bf16[2,8,128,128]{3,2,0,1:T(8,128)(2,1)}), bf16[2,8,512,128]{3,2,0,1:T(8,128)(2,1)}) %all-gather.6.cloned.1.call-update) | async-done | bytes 2097168 | tf_op jit(solution)/shard_map/all_gather | solution.py:110
  152.5 1.4 fusion.175
  153.9 0.5 copy-done.1
  154.4 1.2 fusion.34
  155.6 1.6 collective-permute-start.6
  157.2 1.5 collective-permute-start.7
  158.7 0.3 convolution_add_fusion.2
  159.0 0.3 convolution_add_fusion.1
  159.7 2.8 %collective-permute-done.7 = bf16[2,2,4,128,128]{4,3,0,1,2:T(8,128)(2,1)S(1)} collective-permute-done((bf16[2,2,4,128,128]{4,3,0,1,2:T(8,128)(2,1)S(1)}, bf16[2,2,4,128,128]{4,3,0,1,2:T(8,128)(2,1)S(1)}, u32[]{:S(2)}, u32[]{:S(2)}) %collective-permute-start.7) | collective-permute-done | bytes 524320 | tf_op jit(solution)/shard_map/ppermute | solution.py:15
  162.8 0.3 convolution_add_fusion.5
  163.1 0.3 convolution_add_fusion.4
  163.7 0.7 copy-done.5
  164.5 0.4 fusion.26
  164.9 0.7 copy.136
  165.6 0.8 copy.59
  166.5 60.1 %all-reduce.5.cloned.1.call-done = bf16[2,16384]{1,0:T(2,128)(2,1)} async-done(((bf16[2,16384]{1,0:T(2,128)(2,1)}), bf16[2,16384]{1,0:T(2,128)(2,1)}) %all-reduce.5.cloned.1.call-update) | async-done | bytes 65552 | tf_op jit(solution)/shard_map/psum | solution.py:22
  226.5 7.9 %fusion.31 = f32[1,2,384]{2,1,0:T(2,128)S(1)} fusion(bf16[2,16384]{1,0:T(2,128)(2,1)} %all-reduce.5.cloned.1.call-done, bf16[1,384,1,16384]{3,1,2,0:T(8,128)(2,1)} %param.10), kind=kOutput, calls=%fused_computation.47 | convolution fusion | flops 25165824 | bytes 12651520 | tf_op jit(solution)/shard_map/kfm,fpm->fkp/dot_general | solution.py:125
  234.5 11.7 %psum.15 = f32[1,2,384]{2,1,0:T(2,128)S(1)} all-reduce(f32[1,2,384]{2,1,0:T(2,128)S(1)} %fusion.31), channel_id=1, replica_groups=mesh['aux'=8,'orb'=4] {'orb'}, use_global_device_ids=true, to_apply=%region_1.2 | all-reduce | flops 768 | bytes 6144 | tf_op jit(solution)/shard_map/psum | solution.py:128
  246.2 8.4 %all_gather.11 = f32[1,2,3072]{2,1,0:T(2,128)S(1)} all-gather(f32[1,2,384]{2,1,0:T(2,128)S(1)} %psum.15), channel_id=1, replica_groups=mesh['aux'=8,'orb'=4] {'aux'}, dimensions={2}, use_global_device_ids=true | all-gather | bytes 27648 | tf_op jit(solution)/shard_map/all_gather | solution.py:129
  254.6 6.3 %fusion.28 = f32[1,2,384]{2,1,0:T(2,128)} fusion(f32[1,384,3072]{2,1,0:T(8,128)} %param.11, f32[1,2,3072]{2,1,0:T(2,128)S(1)} %all_gather.11), kind=kOutput, calls=%fused_computation.46 | convolution fusion | flops 28311552 | bytes 4746240 | tf_op jit(solution)/shard_map/fpq,fkq->fkp/dot_general | solution.py:130
  (48 shorter events, 3.1 us)
Async XLA Ops:
  7.2 70.3 %all-gather.4.cloned.1.call-start = ((), (), s32[]{:S(2)}) async-start(), calls=%async_computation | async-start | bytes 3932160 | tf_op jit(solution)/shard_map/all_gather | solution.py:98
  11.2 141.3 %all-gather.6.cloned.1.call-start = ((), (), s32[]{:S(2)}) async-start(), calls=%async_computation.2 | async-start | bytes 2621440 | tf_op jit(solution)/shard_map/all_gather | solution.py:110
  78.8 10.7 %collective-permute-start.2 = (bf16[1,4,4,128,128]{4,3,0,1,2:T(8,128)(2,1)S(1)}, bf16[1,4,4,128,128]{4,3,0,1,2:T(8,128)(2,1)S(1)}, u32[]{:S(2)}, u32[]{:S(2)}) collective-permute-start(bf16[1,4,4,128,128]{4,3,0,1,2:T(8,128)(2,1)S(1)} %get-tuple-element.12), channel_id=1, source_target_pairs={{0,4},{4,8},{8,12},{12,16},{16,20},{20,24},{24,28},{1,5},{5,9},{9,... | collective-permute-start | bytes 1572872 | tf_op jit(solution)/shard_map/ppermute | solution.py:12
  80.4 8.7 %copy-start = (bf16[3,8,4,128,128]{4,3,1,0,2:T(8,128)(2,1)S(1)}, bf16[3,8,4,128,128]{4,3,1,0,2:T(8,128)(2,1)}, u32[]{:S(2)}) copy-start(bf16[3,8,4,128,128]{4,3,1,0,2:T(8,128)(2,1)} %all-gather.4.cloned.1.call-done) | copy-start | bytes 9437188
  80.4 9.0 %collective-permute-start.3 = (bf16[1,4,4,128,128]{4,3,0,1,2:T(8,128)(2,1)S(1)}, bf16[1,4,4,128,128]{4,3,0,1,2:T(8,128)(2,1)S(1)}, u32[]{:S(2)}, u32[]{:S(2)}) collective-permute-start(bf16[1,4,4,128,128]{4,3,0,1,2:T(8,128)(2,1)S(1)} %get-tuple-element.13), channel_id=1, source_target_pairs={{4,0},{8,4},{12,8},{16,12},{20,16},{24,20},{28,24},{5,1},{9,5},{13... | collective-permute-start | bytes 1572872 | tf_op jit(solution)/shard_map/ppermute | solution.py:15
  83.3 11.0 %collective-permute-start = (bf16[2,2,4,128,128]{4,3,0,1,2:T(8,128)(2,1)S(1)}, bf16[2,2,4,128,128]{4,3,0,1,2:T(8,128)(2,1)S(1)}, u32[]{:S(2)}, u32[]{:S(2)}) collective-permute-start(bf16[2,2,4,128,128]{4,3,0,1,2:T(8,128)(2,1)S(1)} %copy.88), channel_id=1, source_target_pairs={{0,4},{4,8},{8,12},{12,16},{16,20},{20,24},{24,28},{1,5},{5,9},{9,... | collective-permute-start | bytes 1572872 | tf_op jit(solution)/shard_map/ppermute | solution.py:12
  87.8 6.8 %collective-permute-start.1 = (bf16[2,2,4,128,128]{4,3,0,1,2:T(8,128)(2,1)S(1)}, bf16[2,2,4,128,128]{4,3,0,1,2:T(8,128)(2,1)S(1)}, u32[]{:S(2)}, u32[]{:S(2)}) collective-permute-start(bf16[2,2,4,128,128]{4,3,0,1,2:T(8,128)(2,1)S(1)} %copy.90), channel_id=1, source_target_pairs={{4,0},{8,4},{12,8},{16,12},{20,16},{24,20},{28,24},{5,1},{9,5},{13... | collective-permute-start | bytes 1572872 | tf_op jit(solution)/shard_map/ppermute | solution.py:15
  89.4 0.8 copy-start.6
  95.9 1.2 copy-start.8
  97.0 129.5 %all-reduce.5.cloned.1.call-start = ((), (), s32[]{:S(2)}) async-start(), calls=%async_computation.1 | async-start | bytes 131072 | tf_op jit(solution)/shard_map/psum | solution.py:22
  97.2 16.2 %collective-permute-start.4 = (s32[2,4]{0,1:T(4,128)S(1)}, s32[2,4]{0,1:T(4,128)S(1)}, u32[]{:S(2)}, u32[]{:S(2)}) collective-permute-start(s32[2,4]{0,1:T(4,128)S(1)} %get-tuple-element.22), channel_id=1, source_target_pairs={{0,4},{4,8},{8,12},{12,16},{16,20},{20,24},{24,28},{1,5},{5,9},{9,... | collective-permute-start | bytes 104 | tf_op jit(solution)/shard_map/ppermute | solution.py:12
  111.3 3.1 %collective-permute-start.5 = (s32[2,4]{0,1:T(4,128)S(1)}, s32[2,4]{0,1:T(4,128)S(1)}, u32[]{:S(2)}, u32[]{:S(2)}) collective-permute-start(s32[2,4]{0,1:T(4,128)S(1)} %get-tuple-element.23), channel_id=1, source_target_pairs={{4,0},{8,4},{12,8},{16,12},{20,16},{24,20},{28,24},{5,1},{9,5},{13... | collective-permute-start | bytes 104 | tf_op jit(solution)/shard_map/ppermute | solution.py:15
  114.6 1.9 copy-start.7
  116.5 1.4 copy-start.3
  117.9 1.4 copy-start.4
  152.5 1.9 copy-start.1
  152.5 6.2 %copy-start.2 = (bf16[12,128,4,128]{3,1,2,0:T(8,128)(2,1)S(1)}, bf16[12,128,4,128]{3,1,2,0:T(8,128)(2,1)}, u32[]{:S(2)}) copy-start(bf16[12,128,4,128]{3,1,2,0:T(8,128)(2,1)} %select_convert_fusion) | copy-start | bytes 4718596
  155.6 3.7 %collective-permute-start.6 = (bf16[2,2,4,128,128]{4,3,0,1,2:T(8,128)(2,1)S(1)}, bf16[2,2,4,128,128]{4,3,0,1,2:T(8,128)(2,1)S(1)}, u32[]{:S(2)}, u32[]{:S(2)}) collective-permute-start(bf16[2,2,4,128,128]{4,3,0,1,2:T(8,128)(2,1)S(1)} %get-tuple-element.21), channel_id=1, source_target_pairs={{0,4},{4,8},{8,12},{12,16},{16,20},{20,24},{24,28},{1,5},{5,9},{9,... | collective-permute-start | bytes 1572872 | tf_op jit(solution)/shard_map/ppermute | solution.py:12
  157.2 5.2 %collective-permute-start.7 = (bf16[2,2,4,128,128]{4,3,0,1,2:T(8,128)(2,1)S(1)}, bf16[2,2,4,128,128]{4,3,0,1,2:T(8,128)(2,1)S(1)}, u32[]{:S(2)}, u32[]{:S(2)}) collective-permute-start(bf16[2,2,4,128,128]{4,3,0,1,2:T(8,128)(2,1)S(1)} %get-tuple-element.20), channel_id=1, source_target_pairs={{4,0},{8,4},{12,8},{16,12},{20,16},{24,20},{28,24},{5,1},{9,5},{13... | collective-permute-start | bytes 1572872 | tf_op jit(solution)/shard_map/ppermute | solution.py:15
  163.4 1.0 copy-start.5
Sparse Core Ops, SparseCore 0:
  11.3 66.1 all-gather.3
  97.2 55.2 all-gather.5
  165.7 60.7 all-reduce.4
where the time goes:
time: 268 us; the launch traced here: 267 us
  waiting for transfers between devices  161 us (60%)
  starting transfers between devices  27.5 us (10%)
  matrix products  25.6 us (10%)
  blocking collectives  20.1 us (8%)
  between operations  14.9 us (6%)
  local copies, waits for them, and re-layouts  14.5 us (5%)
  other arithmetic  3.29 us (1%)
    all_gather x1, waiting for transfers between devices, on_device(): whole_rows = lax.all_gather(stacked, 'orb', axis=2, tiled=True)  66.3 us
    psum x1, waiting for transfers between devices, from_root(): return lax.psum(kept, axis)  60.1 us
    all_gather x1, waiting for transfers between devices, on_device(): lax.all_gather(first_order[:, :, None], 'orb', axis=2, tiled=True)  31.2 us
    ppermute x4, starting transfers between devices, padded_2(): lax.ppermute(lax.slice_in_dim(block, block.shape[dim] - width, None, axis...  21.8 us
    psum x1, blocking collectives, on_device(): summed = lax.psum(partial_value, 'orb')  11.7 us
    all_gather x1, blocking collectives, on_device(): full_sums = lax.all_gather(summed, 'aux', axis=2, tiled=True)  8.42 us
    dot_general x1, matrix products, on_device(): jnp.einsum('kfm,fpm->fkp', flat_blocks, integrals, preferred_element_type...  7.95 us
    unnamed x28, local copies, waits for them, and re-layouts  7.35 us
  transfers between devices with their start and end apart: 11, of which 5 were waited for; matrix products, arithmetic and copies ran while one was open for 5% of the time, Pallas kernels for 0%

commit v1 on v0

--- a/solution.py
+++ b/solution.py
@@ -19,7 +19,7 @@
 
 def from_root(value, axis, source):
     kept = jnp.where(lax.axis_index(axis) == source, value, 0).astype(value.dtype)
-    return lax.psum(kept, axis)
+    return jnp.sum(lax.all_gather(kept, axis), axis=0)
 
 
 def slide_slots(blocks, offset):

time: 268 us -> 220 us (0.82)
  waiting for transfers between devices: 161 us -> 102 us
  blocking collectives: 20.1 us -> 37.1 us
  matrix products: 25.6 us -> 21 us
    psum x1 -> x0, waiting for transfers between devices: 60.1 us -> none  [from_root(): return lax.psum(kept, axis)]
    all_gather x0 -> x1, blocking collectives: none -> 18.9 us  [from_root(): return jnp.sum(lax.all_gather(kept, axis), axis=0)]
    dot_general x1, matrix products: 7.95 us -> 3.34 us  [on_device(): jnp.einsum('kfm,fpm->fkp', flat_blocks, integrals, preferred_element_type...]
    unnamed x28 -> x33, local copies, waits for them, and re-layouts: 7.35 us -> 6.85 us
  transfers between devices with their start and end apart: 11 -> 10, of which waited for: 5 -> 4; matrix products, arithmetic and copies ran while one was open for 5% -> 5% of each run, Pallas kernels for 0% -> 0%
where the time goes in v1:
time: 220 us
  waiting for transfers between devices  102 us (46%)
  blocking collectives  37.1 us (17%)
  starting transfers between devices  27.3 us (12%)
  matrix products  21 us (10%)
  between operations  15.3 us (7%)
  local copies, waits for them, and re-layouts  14 us (6%)
  other arithmetic  3.36 us (2%)
    all_gather x1, waiting for transfers between devices, on_device(): whole_rows = lax.all_gather(stacked, 'orb', axis=2, tiled=True)  66.3 us
    all_gather x1, waiting for transfers between devices, on_device(): lax.all_gather(first_order[:, :, None], 'orb', axis=2, tiled=True)  31.3 us
    ppermute x4, starting transfers between devices, padded_2(): lax.ppermute(lax.slice_in_dim(block, block.shape[dim] - width, None, axis...  21.8 us
    all_gather x1, blocking collectives, from_root(): return jnp.sum(lax.all_gather(kept, axis), axis=0)  18.9 us
    psum x1, blocking collectives, on_device(): summed = lax.psum(partial_value, 'orb')  9.5 us
    all_gather x1, blocking collectives, on_device(): full_sums = lax.all_gather(summed, 'aux', axis=2, tiled=True)  8.68 us
    unnamed x33, local copies, waits for them, and re-layouts  6.85 us
    dot_general x16, matrix products, own_slot_product(): jnp.matmul(factor_left[:, :, stride], picked, preferred_element_type=jnp....  6.57 us
  transfers between devices with their start and end apart: 10, of which 4 were waited for; matrix products, arithmetic and copies ran while one was open for 5% of the time, Pallas kernels for 0%

profile of v1, /device:TPU:0, one launch (start us, length us, event | category | flops | bytes accessed | tf_op | source)
XLA Modules:
  0.0 219.5 jit_solution(2353370560702194222)
XLA Ops:
  7.2 0.7 fusion.142
  7.9 1.1 copy_select_fusion
  9.1 1.0 bitcast_select_fusion
  10.2 0.9 copy.31
  11.2 66.3 %all-gather.5.cloned.1.call-done = bf16[3,8,4,128,128]{4,3,1,0,2:T(8,128)(2,1)} async-done(((bf16[3,8,1,128,128]{4,3,1,0,2:T(8,128)(2,1)}), bf16[3,8,4,128,128]{4,3,1,0,2:T(8,128)(2,1)}) %all-gather.5.cloned.1.call-update) | async-done | bytes 3145744 | tf_op jit(solution)/shard_map/all_gather | solution.py:98
  77.5 1.3 slice_bitcast_fusion.10
  78.8 1.6 collective-permute-start.2
  80.4 1.6 collective-permute-start.3
  82.0 1.3 fusion.175
  83.3 4.5 %collective-permute-start = (bf16[2,2,4,128,128]{4,3,0,1,2:T(8,128)(2,1)S(1)}, bf16[2,2,4,128,128]{4,3,0,1,2:T(8,128)(2,1)S(1)}, u32[]{:S(2)}, u32[]{:S(2)}) collective-permute-start(bf16[2,2,4,128,128]{4,3,0,1,2:T(8,128)(2,1)S(1)} %copy.89), channel_id=1, source_target_pairs={{0,4},{4,8},{8,12},{12,16},{16,20},{20,24},{24,28},{1,5},{5,9},{9,... | collective-permute-start | bytes 1572872 | tf_op jit(solution)/shard_map/ppermute | solution.py:12
  87.8 1.3 collective-permute-start.1
  89.4 0.8 copy-done.6
  90.5 2.9 %fusion.176 = (bf16[1,12,4,128,128]{4,3,0,1,2:T(8,128)(2,1)}, bf16[12,4,128,128]{3,2,0,1:T(8,128)(2,1)}, bf16[1,12,4,128,128]{4,3,0,1,2:T(8,128)(2,1)}, bf16[1,12,4,128,128]{4,3,0,1,2:T(8,128)(2,1)S(1)}) fusion(bf16[1,16,4,128,128]{4,3,0,1,2:T(8,128)(2,1)S(1)} %pad_maximum_fusion), kind=kLoop, calls=%fused_computation.230 | loop fusion | bytes 11010048 | tf_op jit(solution)/shard_map/slice | solution.py:72
  93.7 0.3 convolution_add_fusion.8
  94.0 0.3 convolution_add_fusion.7
  95.0 0.3 convolution_add_fusion.11
  95.3 0.3 convolution_add_fusion.10
  95.6 0.3 fusion.25
  95.9 1.1 fusion.27
  97.1 14.1 %collective-permute-start.4 = (s32[2,4]{0,1:T(4,128)S(1)}, s32[2,4]{0,1:T(4,128)S(1)}, u32[]{:S(2)}, u32[]{:S(2)}) collective-permute-start(s32[2,4]{0,1:T(4,128)S(1)} %get-tuple-element.22), channel_id=1, source_target_pairs={{0,4},{4,8},{8,12},{12,16},{16,20},{20,24},{24,28},{1,5},{5,9},{9,... | collective-permute-start | bytes 104 | tf_op jit(solution)/shard_map/ppermute | solution.py:12
  111.3 1.3 collective-permute-start.5
  113.3 1.0 collective-permute-done.5
  114.5 1.9 fusion.13
  116.4 0.4 fusion.15
  116.9 0.9 copy-done.3
  117.8 0.6 fusion.11
  118.4 0.8 copy-done.4
  119.2 2.0 select_convert_fusion
  121.2 31.3 %all-gather.7.cloned.1.call-done = bf16[2,8,512,128]{3,2,0,1:T(8,128)(2,1)} async-done(((bf16[2,8,128,128]{3,2,0,1:T(8,128)(2,1)}), bf16[2,8,512,128]{3,2,0,1:T(8,128)(2,1)}) %all-gather.7.cloned.1.call-update) | async-done | bytes 2097168 | tf_op jit(solution)/shard_map/all_gather | solution.py:110
  152.5 1.4 fusion.177
  153.9 0.5 copy-done.1
  154.4 1.2 fusion.34
  155.6 1.6 collective-permute-start.6
  157.2 1.3 collective-permute-start.7
  158.6 0.3 convolution_add_fusion.2
  158.9 0.3 convolution_add_fusion.1
  159.5 2.9 %collective-permute-done.7 = bf16[2,2,4,128,128]{4,3,0,1,2:T(8,128)(2,1)S(1)} collective-permute-done((bf16[2,2,4,128,128]{4,3,0,1,2:T(8,128)(2,1)S(1)}, bf16[2,2,4,128,128]{4,3,0,1,2:T(8,128)(2,1)S(1)}, u32[]{:S(2)}, u32[]{:S(2)}) %collective-permute-start.7) | collective-permute-done | bytes 524320 | tf_op jit(solution)/shard_map/ppermute | solution.py:15
  162.8 0.3 convolution_add_fusion.5
  163.1 0.3 convolution_add_fusion.4
  163.4 0.3 fusion.21
  163.7 0.9 copy-done.5
  164.6 0.4 fusion.26
  165.1 18.9 %all-gather.1 = bf16[16,1,128,128]{3,2,1,0:T(8,128)(2,1)S(1)} all-gather(bf16[2,1,128,128]{3,2,1,0:T(8,128)(2,1)S(1)} %select_bitcast_fusion), channel_id=3, replica_groups=mesh['aux'=8,'orb'=4] {'aux'}, dimensions={0}, use_global_device_ids=true | all-gather | bytes 589824 | tf_op jit(solution)/shard_map/all_gather | solution.py:22
  184.1 3.3 %fusion.31 = f32[1,2,384]{2,1,0:T(2,128)S(1)} fusion(bf16[1,384,1,16384]{3,1,2,0:T(8,128)(2,1)S(1)} %bitcast.285, bf16[1,2,128,128]{3,2,1,0:T(8,128)(2,1)S(1)} %bitcast.292), kind=kOutput, calls=%fused_computation.47 | convolution fusion | flops 25165824 | bytes 12651520 | tf_op jit(solution)/shard_map/kfm,fpm->fkp/dot_general | solution.py:125
  187.4 9.5 %psum.7 = f32[1,2,384]{2,1,0:T(2,128)S(1)} all-reduce(f32[1,2,384]{2,1,0:T(2,128)S(1)} %fusion.31), channel_id=1, replica_groups=mesh['aux'=8,'orb'=4] {'orb'}, use_global_device_ids=true, to_apply=%region_1.2 | all-reduce | flops 768 | bytes 6144 | tf_op jit(solution)/shard_map/psum | solution.py:128
  196.9 8.7 %all_gather.19 = f32[1,2,3072]{2,1,0:T(2,128)S(1)} all-gather(f32[1,2,384]{2,1,0:T(2,128)S(1)} %psum.7), channel_id=1, replica_groups=mesh['aux'=8,'orb'=4] {'aux'}, dimensions={2}, use_global_device_ids=true | all-gather | bytes 27648 | tf_op jit(solution)/shard_map/all_gather | solution.py:129
  205.6 0.8 copy.60
  206.4 6.3 %fusion.28 = f32[1,2,384]{2,1,0:T(2,128)} fusion(f32[1,384,3072]{2,1,0:T(8,128)} %param.11, f32[1,2,3072]{2,1,0:T(2,128)S(1)} %all_gather.19), kind=kOutput, calls=%fused_computation.46 | convolution fusion | flops 28311552 | bytes 4746240 | tf_op jit(solution)/shard_map/fpq,fkq->fkp/dot_general | solution.py:130
  (53 shorter events, 2.9 us)
Async XLA Ops:
  7.2 70.3 %all-gather.5.cloned.1.call-start = ((), (), s32[]{:S(2)}) async-start(), calls=%async_computation | async-start | bytes 3932160 | tf_op jit(solution)/shard_map/all_gather | solution.py:98
  11.2 141.3 %all-gather.7.cloned.1.call-start = ((), (), s32[]{:S(2)}) async-start(), calls=%async_computation.1 | async-start | bytes 2621440 | tf_op jit(solution)/shard_map/all_gather | solution.py:110
  78.8 10.7 %collective-permute-start.2 = (bf16[1,4,4,128,128]{4,3,0,1,2:T(8,128)(2,1)S(1)}, bf16[1,4,4,128,128]{4,3,0,1,2:T(8,128)(2,1)S(1)}, u32[]{:S(2)}, u32[]{:S(2)}) collective-permute-start(bf16[1,4,4,128,128]{4,3,0,1,2:T(8,128)(2,1)S(1)} %get-tuple-element.12), channel_id=1, source_target_pairs={{0,4},{4,8},{8,12},{12,16},{16,20},{20,24},{24,28},{1,5},{5,9},{9,... | collective-permute-start | bytes 1572872 | tf_op jit(solution)/shard_map/ppermute | solution.py:12
  80.4 8.7 %copy-start = (bf16[3,8,4,128,128]{4,3,1,0,2:T(8,128)(2,1)S(1)}, bf16[3,8,4,128,128]{4,3,1,0,2:T(8,128)(2,1)}, u32[]{:S(2)}) copy-start(bf16[3,8,4,128,128]{4,3,1,0,2:T(8,128)(2,1)} %all-gather.5.cloned.1.call-done) | copy-start | bytes 9437188
  80.4 9.0 %collective-permute-start.3 = (bf16[1,4,4,128,128]{4,3,0,1,2:T(8,128)(2,1)S(1)}, bf16[1,4,4,128,128]{4,3,0,1,2:T(8,128)(2,1)S(1)}, u32[]{:S(2)}, u32[]{:S(2)}) collective-permute-start(bf16[1,4,4,128,128]{4,3,0,1,2:T(8,128)(2,1)S(1)} %get-tuple-element.13), channel_id=1, source_target_pairs={{4,0},{8,4},{12,8},{16,12},{20,16},{24,20},{28,24},{5,1},{9,5},{13... | collective-permute-start | bytes 1572872 | tf_op jit(solution)/shard_map/ppermute | solution.py:15
  83.3 11.0 %collective-permute-start = (bf16[2,2,4,128,128]{4,3,0,1,2:T(8,128)(2,1)S(1)}, bf16[2,2,4,128,128]{4,3,0,1,2:T(8,128)(2,1)S(1)}, u32[]{:S(2)}, u32[]{:S(2)}) collective-permute-start(bf16[2,2,4,128,128]{4,3,0,1,2:T(8,128)(2,1)S(1)} %copy.89), channel_id=1, source_target_pairs={{0,4},{4,8},{8,12},{12,16},{16,20},{20,24},{24,28},{1,5},{5,9},{9,... | collective-permute-start | bytes 1572872 | tf_op jit(solution)/shard_map/ppermute | solution.py:12
  87.8 6.8 %collective-permute-start.1 = (bf16[2,2,4,128,128]{4,3,0,1,2:T(8,128)(2,1)S(1)}, bf16[2,2,4,128,128]{4,3,0,1,2:T(8,128)(2,1)S(1)}, u32[]{:S(2)}, u32[]{:S(2)}) collective-permute-start(bf16[2,2,4,128,128]{4,3,0,1,2:T(8,128)(2,1)S(1)} %copy.91), channel_id=1, source_target_pairs={{4,0},{8,4},{12,8},{16,12},{20,16},{24,20},{28,24},{5,1},{9,5},{13... | collective-permute-start | bytes 1572872 | tf_op jit(solution)/shard_map/ppermute | solution.py:15
  89.4 0.8 copy-start.6
  95.9 1.2 copy-start.8
  97.1 16.1 %collective-permute-start.4 = (s32[2,4]{0,1:T(4,128)S(1)}, s32[2,4]{0,1:T(4,128)S(1)}, u32[]{:S(2)}, u32[]{:S(2)}) collective-permute-start(s32[2,4]{0,1:T(4,128)S(1)} %get-tuple-element.22), channel_id=1, source_target_pairs={{0,4},{4,8},{8,12},{12,16},{16,20},{20,24},{24,28},{1,5},{5,9},{9,... | collective-permute-start | bytes 104 | tf_op jit(solution)/shard_map/ppermute | solution.py:12
  111.3 3.1 %collective-permute-start.5 = (s32[2,4]{0,1:T(4,128)S(1)}, s32[2,4]{0,1:T(4,128)S(1)}, u32[]{:S(2)}, u32[]{:S(2)}) collective-permute-start(s32[2,4]{0,1:T(4,128)S(1)} %get-tuple-element.23), channel_id=1, source_target_pairs={{4,0},{8,4},{12,8},{16,12},{20,16},{24,20},{28,24},{5,1},{9,5},{13... | collective-permute-start | bytes 104 | tf_op jit(solution)/shard_map/ppermute | solution.py:15
  114.5 1.9 copy-start.7
  116.4 1.4 copy-start.3
  117.8 1.4 copy-start.4
  152.5 1.9 copy-start.1
  152.5 6.1 %copy-start.2 = (bf16[12,128,4,128]{3,1,2,0:T(8,128)(2,1)S(1)}, bf16[12,128,4,128]{3,1,2,0:T(8,128)(2,1)}, u32[]{:S(2)}) copy-start(bf16[12,128,4,128]{3,1,2,0:T(8,128)(2,1)} %select_convert_fusion) | copy-start | bytes 4718596
  155.6 3.5 %collective-permute-start.6 = (bf16[2,2,4,128,128]{4,3,0,1,2:T(8,128)(2,1)S(1)}, bf16[2,2,4,128,128]{4,3,0,1,2:T(8,128)(2,1)S(1)}, u32[]{:S(2)}, u32[]{:S(2)}) collective-permute-start(bf16[2,2,4,128,128]{4,3,0,1,2:T(8,128)(2,1)S(1)} %get-tuple-element.21), channel_id=1, source_target_pairs={{0,4},{4,8},{8,12},{12,16},{16,20},{20,24},{24,28},{1,5},{5,9},{9,... | collective-permute-start | bytes 1572872 | tf_op jit(solution)/shard_map/ppermute | solution.py:12
  157.2 5.2 %collective-permute-start.7 = (bf16[2,2,4,128,128]{4,3,0,1,2:T(8,128)(2,1)S(1)}, bf16[2,2,4,128,128]{4,3,0,1,2:T(8,128)(2,1)S(1)}, u32[]{:S(2)}, u32[]{:S(2)}) collective-permute-start(bf16[2,2,4,128,128]{4,3,0,1,2:T(8,128)(2,1)S(1)} %get-tuple-element.20), channel_id=1, source_target_pairs={{4,0},{8,4},{12,8},{16,12},{20,16},{24,20},{28,24},{5,1},{9,5},{13... | collective-permute-start | bytes 1572872 | tf_op jit(solution)/shard_map/ppermute | solution.py:15
  158.9 25.2 %slice-start = ((s8[12582912]{0:T(1024)(128)(4,1)}), s8[4194304]{0:T(1024)(128)(4,1)S(1)}, s32[]{:S(2)}) async-start(s8[12582912]{0:T(1024)(128)(4,1)} %bitcast.284), calls=%async_computation.2 | async-start | bytes 8388608
  159.5 24.5 %slice-start.1 = ((s8[12582912]{0:T(1024)(128)(4,1)}), s8[4194304]{0:T(1024)(128)(4,1)S(1)}, s32[]{:S(2)}) async-start(s8[12582912]{0:T(1024)(128)(4,1)} %bitcast.284), calls=%async_computation.3 | async-start | bytes 8388608
  163.1 20.9 %slice-start.2 = ((s8[12582912]{0:T(1024)(128)(4,1)}), s8[4194304]{0:T(1024)(128)(4,1)S(1)}, s32[]{:S(2)}) async-start(s8[12582912]{0:T(1024)(128)(4,1)} %bitcast.284), calls=%async_computation.4 | async-start | bytes 8388608
  163.4 1.2 copy-start.5
Sparse Core Ops, SparseCore 0:
  11.3 66.1 all-gather.4
  97.2 55.2 all-gather.6
